TPU v7x, 128 devices: a whole 4x4x4 slice. The times are simulated.
128 devices in a mesh: exp: 16 (over y, z_hi, core), row: 8 (over z_lo, x).
Axes of the slice: x: 4, y: 4, z: 4 (z_hi: 2, z_lo: 2; z = z_hi * 2 + z_lo), core: 2. Of those that a mesh axis runs over, the one named last changes fastest.
Arguments:
- exposures: bfloat16 [16, 39, 128, 2048], P('exp', None, 'row'), may hold values from -6 to 6
- fake_flux: float32 [16, 39, 16], P('exp'), may hold values from -24 to 24
- fake_rows: int32 [16], replicated, may hold values from 0 to 127
- fake_cols: int32 [16], replicated, may hold values from 0 to 2047
- kernel_taps: float32 [39, 16], replicated, may hold values from -0.25 to 0.5
- band_offsets: int32 [39], replicated, may hold values from -12 to -4, as said below
- analysis: bfloat16 [8, 39], replicated, may hold values from -1 to 1
- spectral_basis: bfloat16 [39, 8], replicated, may hold values from -2 to 2
- exposure_weights: float32 [16], replicated, may hold values from -4 to 4
Outputs:
- detection_map: float32 [39, 128, 2048], P(None, 'exp', 'row')
Inputs may be any that keep to these rules, and one draw needn't show every extreme that they name: `band_offsets`: each channel's offset lies in a range such that every output pixel reads pixels at most 12 away; some channel has the smallest offset and some the largest.
All inputs are finite; a program needn't handle non-finite values.
Results may differ from a plain program's by a relative error of at most 0.0065.
Values may be sent and summed in bfloat16 or wider, within the bound.
No kernel may reach another device: no remote copies, remote signals or barrier semaphores. Data moves between devices by JAX's collectives and lax.ppermute only.
A program may use at most 128 MiB of HBM per device.

v0:
```python
import jax
import jax.numpy as jnp
from jax import lax
from jax.sharding import PartitionSpec as P

REACH = 12


def band(tap_values, offsets, count_out, count_in, lead):
    outer = lax.broadcasted_iota(jnp.int32, (count_out, count_in), 0)
    inner = lax.broadcasted_iota(jnp.int32, (count_out, count_in), 1)
    distance = inner[None, :, :] - lead - outer[None, :, :] - offsets[:, None, None]
    matrix = jnp.zeros((tap_values.shape[0], count_out, count_in), jnp.float32)
    for tap_index in range(tap_values.shape[1]):
        weight = tap_values[:, tap_index].astype(jnp.float32)[:, None, None]
        matrix = matrix + jnp.where(distance == tap_index, weight, 0.0)
    return matrix.astype(jnp.bfloat16)


def project(resampled, analysis, spectral_basis):
    coefficients = jnp.einsum(
        "kc,echw->ekhw", analysis, resampled, preferred_element_type=jnp.float32
    ).astype(jnp.bfloat16)
    model = jnp.einsum(
        "ck,ekhw->echw", spectral_basis, coefficients, preferred_element_type=jnp.float32
    )
    return (resampled.astype(jnp.float32) - model).astype(jnp.bfloat16)


def body(
    exposures,
    fake_flux,
    fake_rows,
    fake_cols,
    kernel_taps,
    band_offsets,
    analysis,
    spectral_basis,
    exposure_weights,
):
    local_exp, channels, local_rows, width = exposures.shape
    tap_values = kernel_taps.astype(jnp.bfloat16)
    row_start = lax.axis_index("row") * local_rows
    row_ids = row_start + lax.broadcasted_iota(jnp.int32, (local_rows,), 0)
    col_ids = lax.broadcasted_iota(jnp.int32, (width,), 0)
    row_hits = (fake_rows[:, None] == row_ids[None, :]).astype(jnp.float32)
    col_hits = (fake_cols[:, None] == col_ids[None, :]).astype(jnp.float32)
    added = jnp.einsum(
        "ecf,fh,fw->echw", fake_flux, row_hits, col_hits, precision=lax.Precision.HIGHEST
    )
    injected = (exposures.astype(jnp.float32) + added).astype(jnp.bfloat16)
    block = min(512, width)
    column_kernel = band(tap_values, band_offsets, block, block + 2 * REACH, REACH)
    padded = jnp.pad(injected, ((0, 0), (0, 0), (0, 0), (REACH, REACH)))
    pieces = []
    for block_index in range(width // block):
        window = padded[:, :, :, block_index * block : block_index * block + block + 2 * REACH]
        pieces.append(
            jnp.einsum("echj,cwj->echw", window, column_kernel, preferred_element_type=jnp.float32)
        )
    first = jnp.concatenate(pieces, axis=3).astype(jnp.bfloat16)
    columns = lax.all_to_all(first, "row", split_axis=3, concat_axis=2, tiled=True)
    all_rows = columns.shape[2]
    row_kernel = band(tap_values, band_offsets, all_rows, all_rows, 0)
    second = jnp.einsum(
        "cij,ecjw->eciw", row_kernel, columns, preferred_element_type=jnp.float32
    ).astype(jnp.bfloat16)
    residual = project(second, analysis, spectral_basis)
    total_exp = local_exp * lax.axis_size("exp")
    own_weights = lax.dynamic_slice_in_dim(
        exposure_weights, lax.axis_index("exp") * local_exp, local_exp
    )
    values = residual.astype(jnp.float32)
    first_sum = jnp.sum(values, axis=0)
    weighted_sum = jnp.einsum("e,echw->chw", own_weights, values, precision=lax.Precision.HIGHEST)
    square_sum = jnp.sum(values * values, axis=0)
    first_sum, weighted_sum, square_sum = (
        lax.psum_scatter(first_sum, "exp", scatter_dimension=1, tiled=True),
        lax.psum_scatter(weighted_sum, "exp", scatter_dimension=1, tiled=True),
        lax.psum_scatter(square_sum, "exp", scatter_dimension=1, tiled=True),
    )
    mean_level = first_sum / total_exp
    weighted = weighted_sum - mean_level * jnp.sum(exposure_weights)
    spread = square_sum / total_exp - mean_level * mean_level + 1e-05
    return weighted / jnp.sqrt(total_exp * spread)


def solution(mesh):
    return jax.shard_map(
        body,
        mesh=mesh,
        in_specs=(
            P("exp", None, "row", None),
            P("exp", None, None),
            P(),
            P(),
            P(),
            P(),
            P(),
            P(),
            P(),
        ),
        out_specs=P(None, "exp", "row"),
        check_vma=False,
    )
```

profile of v0, /device:TPU:0, one launch (start us, length us, event | category | flops | bytes accessed | tf_op | source)
XLA Modules:
  0.0 530.4 jit_solution(3733225027252749693)
XLA Ops:
  6.5 0.0 copy-start
  6.5 0.1 iota_subtract_fusion
  6.7 0.7 convert_element_type.229
  7.4 0.7 compare_convert_fusion
  8.1 0.0 copy-start.2
  8.1 6.5 %fusion = bf16[1,39,16,2048]{3,1,2,0:T(8,128)(2,1)S(1)} fusion(bf16[1,39,16,2048]{3,2,1,0:T(8,128)(2,1)} %param.9, s32[16]{0:T(128)} %param.12, f32[16,39]{1,0:T(8,128)} %bitcast.168, f32[16,16]{0,1:T(8,128)S(1)} %compare_convert_fusion), kind=kOutput, calls=%fused_computation.37 | convolution fusion | flops 249243392 | bytes 5115392 | tf_op jit(solution)/shard_map/ecf,fh,fw->echw/dot_general | solution.py:48
  14.6 1.7 fusion.45
  16.3 0.0 copy-done.2
  16.3 70.8 %add_convert_fusion = bf16[39,512,536]{1,2,0:T(8,128)(2,1)} fusion(f32[39]{0:T(128)S(1)} %get-tuple-element.12, f32[39]{0:T(128)S(1)} %get-tuple-element.13, f32[39]{0:T(128)S(1)} %get-tuple-element.14, f32[39]{0:T(128)S(1)} %get-tuple-element.15, f32[39]{0:T(128)S(1)} %get-tuple-element.16, f32[39]{0:T(128)S(1)} %get-tuple-element.17, ...), kind=kLoop, calls=%fused_computation.16 | loop fusion | flops 524439552 | bytes 22506076 | tf_op jit(solution)/shard_map/convert_element_type | solution.py:17
  87.1 8.7 %fusion.42 = bf16[1,39,16,512]{3,2,1,0:T(8,128)(2,1)S(1)} fusion(bf16[39,512,536]{1,2,0:T(8,128)(2,1)} %add_convert_fusion, bf16[39,16,536]{2,0,1:T(8,128)(2,1)S(1)} %get-tuple-element.8), kind=kOutput, calls=%fused_computation.90 | convolution fusion | flops 342810624 | bytes 22713600 | tf_op jit(solution)/shard_map/echj,cwj->echw/dot_general | solution.py:59
  95.8 8.9 %fusion.41 = bf16[1,39,16,512]{3,2,1,0:T(8,128)(2,1)S(1)} fusion(bf16[39,512,536]{1,2,0:T(8,128)(2,1)} %add_convert_fusion, bf16[39,16,536]{2,0,1:T(8,128)(2,1)S(1)} %get-tuple-element.9), kind=kOutput, calls=%fused_computation.89 | convolution fusion | flops 342810624 | bytes 22713600 | tf_op jit(solution)/shard_map/echj,cwj->echw/dot_general | solution.py:59
  104.7 8.7 %fusion.40 = bf16[1,39,16,512]{3,2,1,0:T(8,128)(2,1)S(1)} fusion(bf16[39,512,536]{1,2,0:T(8,128)(2,1)} %add_convert_fusion, bf16[39,16,536]{2,0,1:T(8,128)(2,1)S(1)} %get-tuple-element.10), kind=kOutput, calls=%fused_computation.88 | convolution fusion | flops 342810624 | bytes 22713600 | tf_op jit(solution)/shard_map/echj,cwj->echw/dot_general | solution.py:59
  113.4 8.7 %fusion.39 = bf16[1,39,16,512]{3,2,1,0:T(8,128)(2,1)S(1)} fusion(bf16[39,512,536]{1,2,0:T(8,128)(2,1)} %add_convert_fusion, bf16[39,16,536]{2,0,1:T(8,128)(2,1)S(1)} %get-tuple-element.7), kind=kOutput, calls=%fused_computation.87 | convolution fusion | flops 342810624 | bytes 22713600 | tf_op jit(solution)/shard_map/echj,cwj->echw/dot_general | solution.py:59
  122.1 0.3 pad_maximum_fusion
  122.4 10.2 %copy.62 = bf16[1,39,16,2048]{1,2,0,3:T(8,128)(2,1)} copy(bf16[1,39,16,2048]{3,2,1,0:T(8,128)(2,1)S(1)} %pad_maximum_fusion) | data formatting | bytes 5111808 | tf_op jit(solution)/shard_map/concatenate | solution.py:61
  132.6 16.3 %reshape.268 = bf16[8,2,79872]{2,1,0:T(2,128)(2,1)} reshape(bf16[2048,1,16,39]{3,2,1,0:T(8,128)(2,1)} %bitcast.163) | data formatting | bytes 5111808
  149.0 0.0 copy-start.3
  149.0 5.9 %all-to-all-start = ((bf16[8,2,79872]{2,1,0:T(2,128)(2,1)}), bf16[8,2,79872]{2,1,0:T(2,128)(2,1)S(1)}, u32[]{:S(2)}, u32[]{:S(2)}) async-start(bf16[8,2,79872]{2,1,0:T(2,128)(2,1)} %reshape.268), calls=%async_computation | async-start | bytes 5111808 | tf_op jit(solution)/shard_map/all_to_all | solution.py:62
  154.9 0.0 reduce-scatter.4.cloned.1.call-start
  154.9 0.0 copy-done.3
  154.9 0.6 dynamic_slice.3
  155.5 31.2 %all-to-all-done = bf16[8,2,79872]{2,1,0:T(2,128)(2,1)S(1)} async-done(((bf16[8,2,79872]{2,1,0:T(2,128)(2,1)}), bf16[8,2,79872]{2,1,0:T(2,128)(2,1)S(1)}, u32[]{:S(2)}, u32[]{:S(2)}) %all-to-all-start) | async-done | bytes 2555936 | tf_op jit(solution)/shard_map/all_to_all | solution.py:62
  186.7 24.8 %reshape.269 = bf16[2048,1,16,39]{3,2,1,0:T(8,128)(2,1)} reshape(bf16[8,2,79872]{2,1,0:T(2,128)(2,1)S(1)} %all-to-all-done) | data formatting | bytes 5111808
  211.5 9.8 %copy.73 = bf16[1,39,16,8,256]{4,3,2,1,0:T(8,128)(2,1)S(1)} copy(bf16[1,39,16,8,256]{1,2,4,3,0:T(8,128)(2,1)} %bitcast.164) | data formatting | bytes 5111808 | tf_op jit(solution)/shard_map/all_to_all | solution.py:62
  221.3 0.8 copy.64
  222.1 6.2 %convolution_convert_fusion = bf16[39,256,128]{2,1,0:T(8,128)(2,1)} fusion(bf16[39,128,256]{2,1,0:T(8,128)(2,1)S(1)} %bitcast.167, f32[39]{0:T(128)S(1)} %get-tuple-element.12, f32[39]{0:T(128)S(1)} %get-tuple-element.13, f32[39]{0:T(128)S(1)} %get-tuple-element.14, f32[39]{0:T(128)S(1)} %get-tuple-element.15, f32[39]{0:T(128)S(1)} %get-tuple-element.16, ...), kind=kOutput, calls=%fused_computation.46 | convolution fusion | flops 359743488 | bytes 5179996 | tf_op jit(solution)/shard_map/cij,ecjw->eciw/dot_general | solution.py:65
  228.3 3.8 copy.66
  232.1 0.0 copy-done
  232.1 0.0 copy-done.1
  232.1 3.5 fusion.44
  235.6 6.2 %copy.67 = f32[128,256,39]{0,1,2:T(8,128)} copy(f32[128,256,39]{1,2,0:T(8,128)} %fusion.44) | data formatting | bytes 10223616 | tf_op jit(solution)/shard_map/ck,ekhw->echw/dot_general | solution.py:24
  241.8 7.3 %fusion.1 = (f32[39,128,256]{1,2,0:T(8,128)}, bf16[1,39,128,256]{2,3,1,0:T(8,128)(2,1)S(1)}) fusion(f32[]{:T(128)} %bitcast, f32[128,256,39]{0,1,2:T(8,128)} %copy.67, bf16[39,256,128]{2,1,0:T(8,128)(2,1)} %convolution_convert_fusion), kind=kLoop, calls=%fused_computation.38 | loop fusion | flops 6389760 | bytes 15335428 | tf_op jit(solution)/shard_map/e,echw->chw/dot_general | solution.py:75
  249.1 6.1 %copy.68 = f32[39,128,256]{2,0,1:T(8,128)} copy(f32[39,128,256]{1,2,0:T(8,128)} %get-tuple-element.5) | data formatting | bytes 10223616 | tf_op jit(solution)/shard_map/e,echw->chw/dot_general | solution.py:75
  255.2 0.0 reduce-scatter.4.cloned.1.call-update
  255.2 0.0 reduce-scatter.8.cloned.1.call-start
  255.3 3.0 fusion.2
  258.3 6.1 %copy.70 = f32[39,128,256]{2,0,1:T(8,128)} copy(f32[39,128,256]{1,2,0:T(8,128)} %fusion.2) | data formatting | bytes 10223616 | tf_op jit(solution)/shard_map/reduce_sum | solution.py:76
  264.4 0.0 reduce-scatter.8.cloned.1.call-update
  264.4 0.0 reduce-scatter.6.cloned.1.call-start
  264.5 2.8 convert_bitcast_fusion
  267.3 6.2 %copy.69 = f32[39,128,256]{2,0,1:T(8,128)} copy(f32[39,128,256]{1,2,0:T(8,128)} %convert_bitcast_fusion) | data formatting | bytes 10223616 | tf_op jit(solution)/shard_map/reduce_sum | solution.py:74
  273.5 0.0 reduce-scatter.6.cloned.1.call-update
  273.6 0.6 reduce_sum.16
  274.8 71.2 %reduce-scatter.4.cloned.1.call-done = f32[39,8,256]{2,0,1:T(8,128)} async-done(((f32[39,128,256]{2,0,1:T(8,128)}), f32[39,8,256]{2,0,1:T(8,128)}) %reduce-scatter.4.cloned.1.call-update) | async-done | bytes 319504 | tf_op jit(solution)/shard_map/reduce_scatter | solution.py:79
  346.0 87.9 %reduce-scatter.8.cloned.1.call-done = f32[39,8,256]{2,0,1:T(8,128)} async-done(((f32[39,128,256]{2,0,1:T(8,128)}), f32[39,8,256]{2,0,1:T(8,128)}) %reduce-scatter.8.cloned.1.call-update) | async-done | bytes 319504 | tf_op jit(solution)/shard_map/reduce_scatter | solution.py:80
  433.9 87.9 %reduce-scatter.6.cloned.1.call-done = f32[39,8,256]{2,0,1:T(8,128)} async-done(((f32[39,128,256]{2,0,1:T(8,128)}), f32[39,8,256]{2,0,1:T(8,128)}) %reduce-scatter.6.cloned.1.call-update) | async-done | bytes 319504 | tf_op jit(solution)/shard_map/reduce_scatter | solution.py:78
  521.8 1.3 rsqrt_multiply_fusion
  523.1 0.8 copy.71
  (4 shorter events, 0.0 us)
Async XLA Ops:
  6.5 225.5 %copy-start = (bf16[39,8]{0,1:T(8,128)(2,1)S(1)}, bf16[39,8]{0,1:T(8,128)(2,1)}, u32[]{:S(2)}) copy-start(bf16[39,8]{0,1:T(8,128)(2,1)} %param.16) | copy-start | bytes 1876
  8.1 8.2 %copy-start.2 = (s32[39]{0:T(128)S(1)}, s32[39]{0:T(128)}, u32[]{:S(2)}) copy-start(s32[39]{0:T(128)} %param.14) | copy-start | bytes 472
  149.0 6.0 %copy-start.3 = (f32[16]{0:T(128)S(1)}, f32[16]{0:T(128)}, u32[]{:S(2)}) copy-start(f32[16]{0:T(128)} %param.17) | copy-start | bytes 196
  149.0 37.7 %all-to-all-start = ((bf16[8,2,79872]{2,1,0:T(2,128)(2,1)}), bf16[8,2,79872]{2,1,0:T(2,128)(2,1)S(1)}, u32[]{:S(2)}, u32[]{:S(2)}) async-start(bf16[8,2,79872]{2,1,0:T(2,128)(2,1)} %reshape.268), calls=%async_computation | async-start | bytes 5111808 | tf_op jit(solution)/shard_map/all_to_all | solution.py:62
  154.9 191.1 %reduce-scatter.4.cloned.1.call-start = ((), (), s32[]{:S(2)}) async-start(), calls=%async_computation.4 | async-start | bytes 5570560 | tf_op jit(solution)/shard_map/reduce_scatter | solution.py:79
  228.3 3.8 copy-start.1
  255.2 178.7 %reduce-scatter.8.cloned.1.call-start = ((), (), s32[]{:S(2)}) async-start(), calls=%async_computation.6 | async-start | bytes 5570560 | tf_op jit(solution)/shard_map/reduce_scatter | solution.py:80
  264.4 257.4 %reduce-scatter.6.cloned.1.call-start = ((), (), s32[]{:S(2)}) async-start(), calls=%async_computation.5 | async-start | bytes 5570560 | tf_op jit(solution)/shard_map/reduce_scatter | solution.py:78
Sparse Core Ops, SparseCore 0:
  255.4 90.5 reduce-scatter.3
  350.1 83.8 reduce-scatter.7
  438.0 83.7 reduce-scatter.5
where the time goes:
time: 531 us; the launch traced here: 530 us
  waiting for transfers between devices  278 us (52%)
  local copies, waits for them, and re-layouts  93.5 us (18%)
  other arithmetic  87.6 us (16%)
  matrix products  51.2 us (10%)
  between operations  13.9 us (3%)
  starting transfers between devices  6.02 us (1%)
    reduce_scatter x1, waiting for transfers between devices, body(): lax.psum_scatter(square_sum, 'exp', scatter_dimension=1, tiled=True)  87.9 us
    reduce_scatter x1, waiting for transfers between devices, body(): lax.psum_scatter(first_sum, 'exp', scatter_dimension=1, tiled=True)  87.9 us
    reduce_scatter x1, waiting for transfers between devices, body(): lax.psum_scatter(weighted_sum, 'exp', scatter_dimension=1, tiled=True)  71.2 us
    convert_element_type x1, other arithmetic, band(): return matrix.astype(jnp.bfloat16)  70.8 us
    unnamed x10, local copies, waits for them, and re-layouts  41.1 us
    dot_general x4, matrix products, body(): jnp.einsum('echj,cwj->echw', window, column_kernel, preferred_element_typ...  35 us
    all_to_all x1, waiting for transfers between devices, body(): lax.all_to_all(first, 'row', split_axis=3, concat_axis=2, tiled=True)  31.2 us
  transfers between devices with their start and end apart: 4, of which 4 were waited for; matrix products, arithmetic and copies ran while one was open for 4% of the time, Pallas kernels for 0%

commit v1 on v0

--- a/solution.py
+++ b/solution.py
@@ -59,7 +59,10 @@
             jnp.einsum("echj,cwj->echw", window, column_kernel, preferred_element_type=jnp.float32)
         )
     first = jnp.concatenate(pieces, axis=3).astype(jnp.bfloat16)
-    columns = lax.all_to_all(first, "row", split_axis=3, concat_axis=2, tiled=True)
+    columns = jnp.concatenate(
+        lax.all_to_all(jnp.stack(jnp.split(first, lax.axis_size("row"), axis=3)), "row", 0, 0),
+        axis=2,
+    )
     all_rows = columns.shape[2]
     row_kernel = band(tap_values, band_offsets, all_rows, all_rows, 0)
     second = jnp.einsum(

time: 531 us -> 475 us (0.89)
  local copies, waits for them, and re-layouts: 93.5 us -> 37.8 us
    unnamed x10 -> x15, local copies, waits for them, and re-layouts: 41.1 us -> 5.25 us
    all_to_all x2 -> x0, local copies, waits for them, and re-layouts: 10.6 us -> none  [body(): lax.all_to_all(first, 'row', split_axis=3, concat_axis=2, tiled=True)]
    concatenate x1 -> x0, local copies, waits for them, and re-layouts: 10.2 us -> none  [body(): first = jnp.concatenate(pieces, axis=3).astype(jnp.bfloat16)]
where the time goes in v1:
time: 475 us; the launch traced here: 474 us
  waiting for transfers between devices  278 us (59%)
  other arithmetic  87.4 us (18%)
  matrix products  51.2 us (11%)
  local copies, waits for them, and re-layouts  37.8 us (8%)
  between operations  13.9 us (3%)
  starting transfers between devices  6.02 us (1%)
    reduce_scatter x1, waiting for transfers between devices, body(): lax.psum_scatter(first_sum, 'exp', scatter_dimension=1, tiled=True)  87.8 us
    reduce_scatter x1, waiting for transfers between devices, body(): lax.psum_scatter(square_sum, 'exp', scatter_dimension=1, tiled=True)  87.8 us
    reduce_scatter x1, waiting for transfers between devices, body(): lax.psum_scatter(weighted_sum, 'exp', scatter_dimension=1, tiled=True)  71.2 us
    convert_element_type x1, other arithmetic, band(): return matrix.astype(jnp.bfloat16)  70.8 us
    dot_general x4, matrix products, body(): jnp.einsum('echj,cwj->echw', window, column_kernel, preferred_element_typ...  35 us
    all_to_all x1, waiting for transfers between devices, body(): lax.all_to_all(jnp.stack(jnp.split(first, lax.axis_size('row'), axis=3)),...  31.2 us
  transfers between devices with their start and end apart: 4, of which 4 were waited for; matrix products, arithmetic and copies ran while one was open for 4% of the time, Pallas kernels for 0%

profile of v1, /device:TPU:0, one launch (start us, length us, event | category | flops | bytes accessed | tf_op | source)
XLA Modules:
  0.0 474.4 jit_solution(12559442116831672581)
XLA Ops:
  6.5 0.0 copy-start
  6.5 0.1 iota_subtract_fusion
  6.7 0.7 convert_element_type.229
  7.4 0.7 compare_convert_fusion
  8.1 6.5 %fusion = bf16[1,39,16,2048]{3,1,2,0:T(8,128)(2,1)S(1)} fusion(bf16[1,39,16,2048]{3,2,1,0:T(8,128)(2,1)} %param.9, s32[16]{0:T(128)} %param.12, f32[16,39]{1,0:T(8,128)} %bitcast.195, f32[16,16]{0,1:T(8,128)S(1)} %compare_convert_fusion), kind=kOutput, calls=%fused_computation.37 | convolution fusion | flops 249243392 | bytes 5115392 | tf_op jit(solution)/shard_map/ecf,fh,fw->echw/dot_general | solution.py:48
  14.6 0.0 copy-start.2
  14.6 1.7 fusion.46
  16.3 0.0 copy-done.2
  16.3 70.8 %add_convert_fusion = bf16[39,512,536]{1,2,0:T(8,128)(2,1)} fusion(f32[39]{0:T(128)S(1)} %get-tuple-element.12, f32[39]{0:T(128)S(1)} %get-tuple-element.13, f32[39]{0:T(128)S(1)} %get-tuple-element.14, f32[39]{0:T(128)S(1)} %get-tuple-element.15, f32[39]{0:T(128)S(1)} %get-tuple-element.16, f32[39]{0:T(128)S(1)} %get-tuple-element.17, ...), kind=kLoop, calls=%fused_computation.16 | loop fusion | flops 524439552 | bytes 22506076 | tf_op jit(solution)/shard_map/convert_element_type | solution.py:17
  87.1 8.7 %fusion.42 = bf16[1,39,16,512]{3,2,1,0:T(8,128)(2,1)S(1)} fusion(bf16[39,512,536]{1,2,0:T(8,128)(2,1)} %add_convert_fusion, bf16[39,16,536]{2,0,1:T(8,128)(2,1)S(1)} %get-tuple-element.7), kind=kOutput, calls=%fused_computation.89 | convolution fusion | flops 342810624 | bytes 22713600 | tf_op jit(solution)/shard_map/echj,cwj->echw/dot_general | solution.py:59
  95.8 8.9 %fusion.41 = bf16[1,39,16,512]{3,2,1,0:T(8,128)(2,1)S(1)} fusion(bf16[39,512,536]{1,2,0:T(8,128)(2,1)} %add_convert_fusion, bf16[39,16,536]{2,0,1:T(8,128)(2,1)S(1)} %get-tuple-element.8), kind=kOutput, calls=%fused_computation.88 | convolution fusion | flops 342810624 | bytes 22713600 | tf_op jit(solution)/shard_map/echj,cwj->echw/dot_general | solution.py:59
  104.7 8.7 %fusion.40 = bf16[1,39,16,512]{3,2,1,0:T(8,128)(2,1)S(1)} fusion(bf16[39,512,536]{1,2,0:T(8,128)(2,1)} %add_convert_fusion, bf16[39,16,536]{2,0,1:T(8,128)(2,1)S(1)} %get-tuple-element.9), kind=kOutput, calls=%fused_computation.87 | convolution fusion | flops 342810624 | bytes 22713600 | tf_op jit(solution)/shard_map/echj,cwj->echw/dot_general | solution.py:59
  113.4 8.7 %fusion.39 = bf16[1,39,16,512]{3,2,1,0:T(8,128)(2,1)S(1)} fusion(bf16[39,512,536]{1,2,0:T(8,128)(2,1)} %add_convert_fusion, bf16[39,16,536]{2,0,1:T(8,128)(2,1)S(1)} %get-tuple-element.10), kind=kOutput, calls=%fused_computation.86 | convolution fusion | flops 342810624 | bytes 22713600 | tf_op jit(solution)/shard_map/echj,cwj->echw/dot_general | solution.py:59
  122.1 0.8 fusion.58
  122.9 0.7 fusion.57
  123.7 0.7 fusion.56
  124.4 0.7 fusion.55
  125.1 0.7 fusion.54
  125.9 0.7 fusion.53
  126.6 0.8 fusion.52
  127.4 0.7 fusion.51
  128.1 5.9 %all-to-all-start = ((bf16[8,1,39,16,256]{4,3,2,1,0:T(8,128)(2,1)}), bf16[8,1,39,16,256]{4,3,2,1,0:T(8,128)(2,1)S(1)}, u32[]{:S(2)}, u32[]{:S(2)}) async-start(bf16[8,1,39,16,256]{4,3,2,1,0:T(8,128)(2,1)} %fusion.51), calls=%async_computation | async-start | bytes 5111808 | tf_op jit(solution)/shard_map/all_to_all | solution.py:63
  134.0 0.0 reduce-scatter.4.cloned.1.call-start
  134.1 0.0 copy-done.3
  134.1 0.6 dynamic_slice.3
  134.7 31.2 %all-to-all-done = bf16[8,1,39,16,256]{4,3,2,1,0:T(8,128)(2,1)S(1)} async-done(((bf16[8,1,39,16,256]{4,3,2,1,0:T(8,128)(2,1)}), bf16[8,1,39,16,256]{4,3,2,1,0:T(8,128)(2,1)S(1)}, u32[]{:S(2)}, u32[]{:S(2)}) %all-to-all-start) | async-done | bytes 2555936 | tf_op jit(solution)/shard_map/all_to_all | solution.py:63
  165.9 0.3 copy.33
  166.2 6.2 %convolution_convert_fusion = bf16[39,256,128]{2,1,0:T(8,128)(2,1)} fusion(bf16[39,128,256]{2,1,0:T(8,128)(2,1)S(1)} %bitcast.194, f32[39]{0:T(128)S(1)} %get-tuple-element.12, f32[39]{0:T(128)S(1)} %get-tuple-element.13, f32[39]{0:T(128)S(1)} %get-tuple-element.14, f32[39]{0:T(128)S(1)} %get-tuple-element.15, f32[39]{0:T(128)S(1)} %get-tuple-element.16, ...), kind=kOutput, calls=%fused_computation.45 | convolution fusion | flops 359743488 | bytes 5179996 | tf_op jit(solution)/shard_map/cij,ecjw->eciw/dot_general | solution.py:68
  172.4 3.8 copy.35
  176.2 3.5 fusion.44
  179.6 6.2 %copy.36 = f32[128,256,39]{0,1,2:T(8,128)} copy(f32[128,256,39]{1,2,0:T(8,128)} %fusion.44) | data formatting | bytes 10223616 | tf_op jit(solution)/shard_map/ck,ekhw->echw/dot_general | solution.py:24
  185.9 7.3 %fusion.1 = (f32[39,128,256]{1,2,0:T(8,128)}, bf16[1,39,128,256]{2,3,1,0:T(8,128)(2,1)S(1)}) fusion(f32[]{:T(128)} %bitcast, f32[128,256,39]{0,1,2:T(8,128)} %copy.36, bf16[39,256,128]{2,1,0:T(8,128)(2,1)} %convolution_convert_fusion), kind=kLoop, calls=%fused_computation.38 | loop fusion | flops 6389760 | bytes 15335428 | tf_op jit(solution)/shard_map/e,echw->chw/dot_general | solution.py:78
  193.2 6.1 %copy.37 = f32[39,128,256]{2,0,1:T(8,128)} copy(f32[39,128,256]{1,2,0:T(8,128)} %get-tuple-element.5) | data formatting | bytes 10223616 | tf_op jit(solution)/shard_map/e,echw->chw/dot_general | solution.py:78
  199.3 0.0 reduce-scatter.4.cloned.1.call-update
  199.3 0.0 reduce-scatter.8.cloned.1.call-start
  199.4 3.0 fusion.2
  202.3 6.1 %copy.39 = f32[39,128,256]{2,0,1:T(8,128)} copy(f32[39,128,256]{1,2,0:T(8,128)} %fusion.2) | data formatting | bytes 10223616 | tf_op jit(solution)/shard_map/reduce_sum | solution.py:79
  208.5 0.0 reduce-scatter.8.cloned.1.call-update
  208.5 0.0 reduce-scatter.6.cloned.1.call-start
  208.6 2.8 convert_bitcast_fusion
  211.4 6.2 %copy.38 = f32[39,128,256]{2,0,1:T(8,128)} copy(f32[39,128,256]{1,2,0:T(8,128)} %convert_bitcast_fusion) | data formatting | bytes 10223616 | tf_op jit(solution)/shard_map/reduce_sum | solution.py:77
  217.6 0.0 reduce-scatter.6.cloned.1.call-update
  217.6 0.6 reduce_sum.16
  218.9 71.2 %reduce-scatter.4.cloned.1.call-done = f32[39,8,256]{2,0,1:T(8,128)} async-done(((f32[39,128,256]{2,0,1:T(8,128)}), f32[39,8,256]{2,0,1:T(8,128)}) %reduce-scatter.4.cloned.1.call-update) | async-done | bytes 319504 | tf_op jit(solution)/shard_map/reduce_scatter | solution.py:82
  290.1 87.8 %reduce-scatter.8.cloned.1.call-done = f32[39,8,256]{2,0,1:T(8,128)} async-done(((f32[39,128,256]{2,0,1:T(8,128)}), f32[39,8,256]{2,0,1:T(8,128)}) %reduce-scatter.8.cloned.1.call-update) | async-done | bytes 319504 | tf_op jit(solution)/shard_map/reduce_scatter | solution.py:83
  377.9 87.8 %reduce-scatter.6.cloned.1.call-done = f32[39,8,256]{2,0,1:T(8,128)} async-done(((f32[39,128,256]{2,0,1:T(8,128)}), f32[39,8,256]{2,0,1:T(8,128)}) %reduce-scatter.6.cloned.1.call-update) | async-done | bytes 319504 | tf_op jit(solution)/shard_map/reduce_scatter | solution.py:81
  465.8 1.3 rsqrt_multiply_fusion
  467.0 0.8 copy.40
  (7 shorter events, 0.0 us)
Async XLA Ops:
  6.5 169.6 %copy-start = (bf16[39,8]{0,1:T(8,128)(2,1)S(1)}, bf16[39,8]{0,1:T(8,128)(2,1)}, u32[]{:S(2)}) copy-start(bf16[39,8]{0,1:T(8,128)(2,1)} %param.16) | copy-start | bytes 1876
  14.6 1.7 copy-start.2
  128.1 6.0 %copy-start.3 = (f32[16]{0:T(128)S(1)}, f32[16]{0:T(128)}, u32[]{:S(2)}) copy-start(f32[16]{0:T(128)} %param.17) | copy-start | bytes 196
  128.1 37.7 %all-to-all-start = ((bf16[8,1,39,16,256]{4,3,2,1,0:T(8,128)(2,1)}), bf16[8,1,39,16,256]{4,3,2,1,0:T(8,128)(2,1)S(1)}, u32[]{:S(2)}, u32[]{:S(2)}) async-start(bf16[8,1,39,16,256]{4,3,2,1,0:T(8,128)(2,1)} %fusion.51), calls=%async_computation | async-start | bytes 5111808 | tf_op jit(solution)/shard_map/all_to_all | solution.py:63
  134.0 156.1 %reduce-scatter.4.cloned.1.call-start = ((), (), s32[]{:S(2)}) async-start(), calls=%async_computation.4 | async-start | bytes 5570560 | tf_op jit(solution)/shard_map/reduce_scatter | solution.py:82
  172.4 3.8 copy-start.1
  199.3 178.6 %reduce-scatter.8.cloned.1.call-start = ((), (), s32[]{:S(2)}) async-start(), calls=%async_computation.6 | async-start | bytes 5570560 | tf_op jit(solution)/shard_map/reduce_scatter | solution.py:83
  208.5 257.2 %reduce-scatter.6.cloned.1.call-start = ((), (), s32[]{:S(2)}) async-start(), calls=%async_computation.5 | async-start | bytes 5570560 | tf_op jit(solution)/shard_map/reduce_scatter | solution.py:81
Sparse Core Ops, SparseCore 0:
  199.4 90.5 reduce-scatter.3
  294.2 83.7 reduce-scatter.7
  382.0 83.7 reduce-scatter.5
